TPU v7x, 32 devices: a whole 2x2x4 slice. The times are simulated.
32 devices in a mesh: tile: 4 (over y, core), dp: 8 (over z, x).
Axes of the slice: x: 2, y: 2, z: 4, core: 2. Of those that a mesh axis runs over, the one named last changes fastest.
Arguments:
- observed: float32 [8, 2, 8, 32], P('dp', None, 'tile'), may hold values from -6 to 6
- targets: float32 [8, 2, 8, 32], P('dp', None, 'tile'), may hold values from -6 to 6
- pixel_mask: int32 [8, 2, 8, 32], P('dp', None, 'tile'), may hold values 0 or 1
- lengths: int32 [8], P('dp'), may hold values from 1 to 2, as said below
- step_count: int32 [1], replicated, may hold values from 2 to 20
- kernels: float32 [1, 12800, 1024], P(None, 'dp'), may hold values from -0.0546875 to 0.0546875
- kernel_moment: float32 [1, 12800, 1024], P(None, 'dp'), may hold values from -7.6293945e-06 to 7.6293945e-06
- kernel_second: float32 [1, 12800, 1024], P(None, 'dp'), may hold values from 1.9073486e-12 to 7.6293945e-12
- norm_params: float32 [2, 1, 1024], replicated
- norm_moment: float32 [2, 1, 1024], replicated, may hold values from -1.5258789e-05 to 1.5258789e-05
- norm_second: float32 [2, 1, 1024], replicated, may hold values from 7.6293945e-12 to 3.0517578e-11
- end_params: float32 [3, 256], replicated
- end_moment: float32 [3, 256], replicated, may hold values from -7.6293945e-05 to 7.6293945e-05
- end_second: float32 [3, 256], replicated, may hold values from 1.9073486e-10 to 7.6293943e-10
- head_bias: float32 [1], replicated, may hold values from -3 to 3
- head_moment: float32 [1], replicated, may hold values from -0.0546875 to 0.0546875
- head_second: float32 [1], replicated, may hold values from 7.6293945e-05 to 0.00030517578
- hidden_init: float32 [1, 8, 8, 32, 256], P(None, 'dp', 'tile'), may hold values from -0.9 to 0.9
- cells_init: float32 [1, 8, 8, 32, 256], P(None, 'dp', 'tile'), may hold values from -5 to 5
Outputs:
- loss_value: float32 [], replicated
- grad_norm: float32 [], replicated
- kernels_new: float32 [1, 12800, 1024], P(None, 'dp')
- kernel_moment_new: float32 [1, 12800, 1024], P(None, 'dp')
- kernel_second_new: float32 [1, 12800, 1024], P(None, 'dp')
- norm_new: float32 [2, 1, 1024], replicated
- norm_moment_new: float32 [2, 1, 1024], replicated
- norm_second_new: float32 [2, 1, 1024], replicated
- end_new: float32 [3, 256], replicated
- end_moment_new: float32 [3, 256], replicated
- end_second_new: float32 [3, 256], replicated
- head_new: float32 [1], replicated
- head_moment_new: float32 [1], replicated
- head_second_new: float32 [1], replicated
- hidden_final: float32 [1, 8, 8, 32, 256], P(None, 'dp', 'tile')
- cells_final: float32 [1, 8, 8, 32, 256], P(None, 'dp', 'tile')
Inputs may be any that keep to these rules, and one draw needn't show every extreme that they name: `lengths`: some stream has all 2 frames counting and some only one.
All inputs are finite; a program needn't handle non-finite values. No bound on the sum of `pixel_mask` on one device may be relied on, other than what follows from the above.
Results may differ from a plain program's by a relative error of at most 0.0003.
The roundings to bfloat16 on the way count: a program that leaves them out, or rounds other values in their place, can miss the bound.
Values may be sent and summed in bfloat16 or wider, within the bound.
No kernel may reach another device: no remote copies, remote signals or barrier semaphores. Data moves between devices by JAX's collectives and lax.ppermute only.
A program may use at most 192 MiB of HBM per device.

v0:
```python
import jax
import jax.numpy as jnp
from jax import lax
from jax.sharding import PartitionSpec as P

IN_DIM = 512
KERNEL = 5
GROUP_SIZE = 64
clip_limit = 0.005
small_rate = 0.1


def padded_2(cells, sides, width):
    for axis, dim in sides:
        count = lax.axis_size(axis)
        ends = count - 1
        head = lax.slice_in_dim(cells, 0, width, axis=dim)
        tail = lax.slice_in_dim(cells, cells.shape[dim] - width, cells.shape[dim], axis=dim)
        cells = jnp.concatenate(
            [
                lax.ppermute(tail, axis, [(i, (i + 1) % count) for i in range(ends)]),
                cells,
                lax.ppermute(head, axis, [((i + 1) % count, i) for i in range(ends)]),
            ],
            axis=dim,
        )
    return cells


def group_norm(gates, gain, shift):
    full_shape = gates.shape
    grouped = gates.reshape(full_shape[:-1] + (full_shape[-1] // GROUP_SIZE, GROUP_SIZE))
    centred = grouped - jnp.mean(grouped, axis=-1, keepdims=True)
    spread = jnp.mean(centred * centred, axis=-1, keepdims=True)
    return (centred * lax.rsqrt(spread + 1e-05)).reshape(full_shape) * gain + shift


def lstm_cell(gates, cells_prev, gain, shift):
    normed = group_norm(gates, gain, shift)
    quarter = normed.shape[-1] // 4
    input_gate = jax.nn.sigmoid(normed[..., :quarter])
    forget_gate = jax.nn.sigmoid(normed[..., quarter : 2 * quarter])
    candidate = jnp.tanh(normed[..., 2 * quarter : 3 * quarter])
    output_gate = jax.nn.sigmoid(normed[..., 3 * quarter :])
    cells_next = forget_gate * cells_prev + input_gate * candidate
    return (output_gate * jnp.tanh(cells_next), cells_next)


def unfold(padded, rows, columns):
    pieces = []
    for row_off in range(KERNEL):
        for col_off in range(KERNEL):
            pieces.append(padded[:, row_off : row_off + rows, col_off : col_off + columns, :])
    joined = jnp.concatenate(pieces, axis=-1)
    return joined.reshape(-1, joined.shape[-1])


def pad_columns(values):
    margin = KERNEL // 2
    return jnp.pad(values, ((0, 0), (0, 0), (margin, margin), (0, 0)))


def layer_forward(weight_full, gain, shift, inputs_low, hidden_start, cells_start):
    rows, columns = (hidden_start.shape[1], hidden_start.shape[2])
    hidden_low = hidden_start.astype(jnp.bfloat16)
    cells = cells_start
    kept = []
    outputs = []
    outputs_low = []
    hidden = hidden_start
    for frame_no in range(len(inputs_low)):
        joined = jnp.concatenate([inputs_low[frame_no], hidden_low], axis=-1)
        padded = padded_2(joined, (("tile", 1),), KERNEL // 2)
        padded = pad_columns(padded)
        gates = jnp.dot(
            unfold(padded, rows, columns), weight_full, preferred_element_type=jnp.float32
        )
        gates = gates.reshape(hidden_start.shape[:3] + (weight_full.shape[1],))
        kept.append((padded, gates, cells))
        hidden, cells = lstm_cell(gates, cells, gain, shift)
        hidden_low = hidden.astype(jnp.bfloat16)
        outputs.append(hidden)
        outputs_low.append(hidden_low)
    return (outputs, outputs_low, kept, hidden, cells)


def layer_backward(weight_full, gain, shift, kept, grad_above):
    pixel_shape = kept[0][1].shape
    rows, columns, gate_dim = (pixel_shape[1], pixel_shape[2], pixel_shape[3])
    in_dim = weight_full.shape[0] // (KERNEL * KERNEL)
    half = in_dim // 2
    flipped = weight_full.reshape(KERNEL, KERNEL, in_dim, gate_dim)[::-1, ::-1]
    flipped = flipped.transpose(0, 1, 3, 2).reshape(KERNEL * KERNEL * gate_dim, in_dim)
    grad_weight = jnp.zeros(weight_full.shape, jnp.float32)
    grad_gain = jnp.zeros(gain.shape, jnp.float32)
    grad_shift = jnp.zeros(shift.shape, jnp.float32)
    grad_hidden = jnp.zeros(pixel_shape[:3] + (half,), jnp.float32)
    grad_cells = jnp.zeros(pixel_shape[:3] + (half,), jnp.float32)
    grad_inputs = [None] * len(kept)
    for frame_no in reversed(range(len(kept))):
        padded, gates, cells_prev = kept[frame_no]
        unused, pull = jax.vjp(lstm_cell, gates, cells_prev, gain, shift)
        grad_gates, grad_cells, part_gain, part_shift = pull(
            (grad_above[frame_no] + grad_hidden, grad_cells)
        )
        grad_gain = grad_gain + part_gain
        grad_shift = grad_shift + part_shift
        gates_low = grad_gates.astype(jnp.bfloat16)
        grad_weight = grad_weight + lax.dot_general(
            unfold(padded, rows, columns),
            gates_low.reshape(-1, gate_dim),
            (((0,), (0,)), ((), ())),
            preferred_element_type=jnp.float32,
        )
        spread = padded_2(gates_low, (("tile", 1),), KERNEL // 2)
        spread = pad_columns(spread)
        grad_joined = jnp.dot(
            unfold(spread, rows, columns), flipped, preferred_element_type=jnp.float32
        )
        grad_joined = grad_joined.reshape(pixel_shape[:3] + (in_dim,))
        grad_inputs[frame_no] = grad_joined[..., :half]
        grad_hidden = grad_joined[..., half:]
    return (grad_weight, grad_gain, grad_shift, grad_inputs)


def adamw(weight, moment, second, grad, rate, correction):
    moment_new = 0.5 * moment + 0.5 * grad
    second_new = 0.5 * second + 0.5 * grad * grad
    update = moment_new / correction / (jnp.sqrt(second_new / correction) + 1e-08)
    return (weight - rate * (update + 0.01 * weight), moment_new, second_new)


def per_device(
    observed,
    targets,
    pixel_mask,
    lengths,
    step_count,
    kernels,
    kernel_moment,
    kernel_second,
    norm_params,
    norm_moment,
    norm_second,
    end_params,
    end_moment,
    end_second,
    head_bias,
    head_moment,
    head_second,
    hidden_init,
    cells_init,
):
    frame_total = observed.shape[1]
    layers = kernels.shape[0]
    frame_ids = lax.broadcasted_iota(jnp.int32, (1, frame_total), 1)
    counted = (frame_ids < lengths[:, None]).astype(jnp.float32)
    valid = pixel_mask.astype(jnp.float32) * counted[:, :, None, None]
    count = jnp.maximum(lax.psum(jnp.sum(valid), ("tile", "dp")), 1.0)
    inputs_low = [
        (end_params[0] * observed[:, frame_no, :, :, None] + end_params[1]).astype(jnp.bfloat16)
        for frame_no in range(frame_total)
    ]
    outputs = []
    layer_no = 0
    weight_full = lax.all_gather(kernels[layer_no].astype(jnp.bfloat16), "dp", axis=0, tiled=True)
    outputs, outputs_low, kept, hidden, cells = layer_forward(
        weight_full,
        norm_params[0, layer_no],
        norm_params[1, layer_no],
        inputs_low,
        hidden_init[layer_no],
        cells_init[layer_no],
    )
    stored_kept = [kept]
    hidden_list = [hidden]
    cells_list = [cells]
    loss_sum = jnp.zeros((), jnp.float32)
    grad_head_weight = jnp.zeros(end_params.shape[1:], jnp.float32)
    grad_head = jnp.zeros((1,), jnp.float32)
    grad_above = []
    for frame_no in range(frame_total):
        predicted = jnp.sum(outputs[frame_no] * end_params[2], axis=-1) + head_bias[0]
        error = predicted - targets[:, frame_no]
        weighted = valid[:, frame_no] * error
        loss_sum = loss_sum + jnp.sum(weighted * error)
        grad_pred = 2.0 * weighted / count
        grad_head = grad_head + jnp.sum(grad_pred)
        grad_head_weight = grad_head_weight + jnp.sum(
            grad_pred[..., None] * outputs[frame_no], axis=(0, 1, 2)
        )
        grad_above.append(grad_pred[..., None] * end_params[2])
    kernel_grads = [None] * layers
    gain_grads = [None] * layers
    shift_grads = [None] * layers
    for layer_no in reversed(range(layers)):
        weight_full = lax.all_gather(
            kernels[layer_no].astype(jnp.bfloat16), "dp", axis=0, tiled=True
        )
        grad_weight, grad_gain, grad_shift, grad_inputs = layer_backward(
            weight_full,
            norm_params[0, layer_no],
            norm_params[1, layer_no],
            stored_kept[layer_no],
            grad_above,
        )
        kernel_grads[layer_no] = grad_weight
        gain_grads[layer_no] = grad_gain
        shift_grads[layer_no] = grad_shift
        grad_above = grad_inputs
    grad_lift_weight = jnp.zeros(end_params.shape[1:], jnp.float32)
    grad_lift_bias = jnp.zeros(end_params.shape[1:], jnp.float32)
    for frame_no in range(frame_total):
        grad_lift_weight = grad_lift_weight + jnp.sum(
            grad_above[frame_no] * observed[:, frame_no, :, :, None], axis=(0, 1, 2)
        )
        grad_lift_bias = grad_lift_bias + jnp.sum(grad_above[frame_no], axis=(0, 1, 2))
    grad_norms = jnp.stack([jnp.stack(gain_grads), jnp.stack(shift_grads)])
    grad_ends = jnp.stack([grad_lift_weight, grad_lift_bias, grad_head_weight])
    grad_kernels = jnp.stack(kernel_grads)
    shard = lax.psum_scatter(grad_kernels, "dp", scatter_dimension=1, tiled=True)
    shard = lax.psum(shard, "tile")
    local_square = jnp.sum(shard * shard)
    grad_norms, grad_ends, grad_head, loss_sum = lax.psum(
        (grad_norms, grad_ends, grad_head, loss_sum), ("tile", "dp")
    )
    kernel_square = lax.psum(local_square, "dp")
    squares = (
        kernel_square
        + jnp.sum(grad_norms * grad_norms)
        + jnp.sum(grad_ends * grad_ends)
        + jnp.sum(grad_head * grad_head)
    )
    grad_norm = jnp.sqrt(squares)
    factor = clip_limit / jnp.maximum(grad_norm, clip_limit)
    correction = 1.0 - jnp.power(0.5, step_count[0].astype(jnp.float32))
    kernel_rate = (KERNEL * KERNEL * IN_DIM) ** (-0.5)
    kern_out = adamw(kernels, kernel_moment, kernel_second, shard * factor, kernel_rate, correction)
    norm_out = adamw(
        norm_params, norm_moment, norm_second, grad_norms * factor, small_rate, correction
    )
    end_out = adamw(end_params, end_moment, end_second, grad_ends * factor, small_rate, correction)
    head_out = adamw(
        head_bias, head_moment, head_second, grad_head * factor, small_rate, correction
    )
    loss_value = loss_sum / count
    return (
        loss_value,
        grad_norm,
        kern_out[0],
        kern_out[1],
        kern_out[2],
        norm_out[0],
        norm_out[1],
        norm_out[2],
        end_out[0],
        end_out[1],
        end_out[2],
        head_out[0],
        head_out[1],
        head_out[2],
        jnp.stack(hidden_list),
        jnp.stack(cells_list),
    )


def solution(mesh):
    placed = (
        P("dp", None, "tile", None),
        P("dp", None, "tile", None),
        P("dp", None, "tile", None),
        P("dp"),
        P(),
        P(None, "dp", None),
        P(None, "dp", None),
        P(None, "dp", None),
        P(),
        P(),
        P(),
        P(),
        P(),
        P(),
        P(),
        P(),
        P(),
        P(None, "dp", "tile", None, None),
        P(None, "dp", "tile", None, None),
    )
    return jax.shard_map(
        per_device,
        mesh=mesh,
        in_specs=placed,
        out_specs=(
            P(),
            P(),
            P(None, "dp", None),
            P(None, "dp", None),
            P(None, "dp", None),
            P(),
            P(),
            P(),
            P(),
            P(),
            P(),
            P(),
            P(),
            P(),
            P(None, "dp", "tile", None, None),
            P(None, "dp", "tile", None, None),
        ),
        check_vma=False,
    )
```

profile of v0, /device:TPU:0, one launch (start us, length us, event | category | flops | bytes accessed | tf_op | source)
XLA Modules:
  0.0 1688.5 jit_solution(5633768059832277343)
XLA Ops:
  7.2 5.1 convert_element_type.95
  13.2 1.3 collective-permute-start.1
  14.5 3.0 collective-permute-start
  18.9 85.6 %psum.50 = f32[]{:T(128)} all-reduce(f32[]{:T(128)} %get-tuple-element.65), channel_id=1, replica_groups=mesh['tile'=4,'dp'=8] {'tile','dp'}, use_global_device_ids=true, to_apply=%region_10.11 | all-reduce | flops 1 | bytes 8 | tf_op jit(solution)/shard_map/psum | solution.py:159
  108.5 408.1 %all-gather.3.cloned.1.call-done = bf16[1,12800,1024]{2,1,0:T(8,128)(2,1)} async-done(((bf16[1,1600,1024]{2,1,0:T(8,128)(2,1)}), bf16[1,12800,1024]{2,1,0:T(8,128)(2,1)}) %all-gather.3.cloned.1.call-update) | async-done | bytes 26214416 | tf_op jit(solution)/shard_map/all_gather | solution.py:166
  516.7 10.8 fusion.3
  530.1 1.3 collective-permute-start.3
  531.4 3.0 collective-permute-start.2
  534.4 18.4 %reverse_bitcast_fusion = bf16[5,5,1024,512]{2,3,1,0:T(8,128)(2,1)} fusion(bf16[5,5,512,1024]{3,2,1,0:T(8,128)(2,1)} %bitcast.214), kind=kLoop, calls=%fused_computation.6 | loop fusion | bytes 52428800 | tf_op jit(solution)/shard_map/transpose | solution.py:93
  552.8 33.9 %copy.35 = bf16[5,5,1024,512]{3,2,1,0:T(8,128)(2,1)} copy(bf16[5,5,1024,512]{2,3,1,0:T(8,128)(2,1)} %reverse_bitcast_fusion) | data formatting | bytes 52428800 | tf_op jit(solution)/shard_map/transpose | solution.py:93
  588.8 10.8 fusion.1
  606.1 1.3 collective-permute-start.5
  607.4 3.8 collective-permute-start.4
  611.2 21.6 %fusion.11 = f32[12800,1024,1]{1,0,2:T(8,128)} fusion(bf16[1,2,32,12800]{3,2,1,0:T(8,128)(2,1)} %copy-done, bf16[1,2,32,1024]{3,2,1,0:T(8,128)(2,1)S(1)} %fusion.25), kind=kOutput, calls=%fused_computation.17 | convolution fusion | flops 1677721600 | bytes 54198272 | tf_op jit(solution)/shard_map/dot_general | solution.py:109
  633.8 10.8 fusion.13
  647.9 33.5 %fusion = f32[1,12800,1024]{2,1,0:T(8,128)} fusion(f32[12800,1024,1]{1,0,2:T(8,128)} %fusion.11, bf16[1,2,32,12800]{3,2,1,0:T(8,128)(2,1)S(1)} %copy-done.2, bf16[1,2,32,1024]{3,2,1,0:T(8,128)(2,1)S(1)} %fusion.27), kind=kOutput, calls=%fused_computation.1 | convolution fusion | flops 1690828800 | bytes 106627072 | tf_op jit(solution)/shard_map/dot_general | solution.py:109
  684.8 4.5 collective-permute-start.6
  705.7 793.9 %reduce-scatter.2.cloned.1.call-done = f32[1,1600,1024]{2,1,0:T(8,128)} async-done(((f32[1,12800,1024]{2,1,0:T(8,128)}), f32[1,1600,1024]{2,1,0:T(8,128)}) %reduce-scatter.2.cloned.1.call-update) | async-done | bytes 6553616 | tf_op jit(solution)/shard_map/reduce_scatter | solution.py:221
  1503.7 12.9 fusion.16
  1516.8 41.4 %all-reduce.12 = (f32[]{:T(128)}, f32[2,1,1024]{2,1,0:T(1,128)S(1)}, f32[3,256]{1,0:T(4,128)S(1)}, f32[1]{0:T(128)}) all-reduce(f32[]{:T(128)S(6)} %add.410, f32[2,1,1024]{2,1,0:T(1,128)S(1)} %pad_maximum_fusion.14, f32[3,256]{1,0:T(4,128)S(1)} %pad_maximum_fusion.15, f32[1]{0:T(128)} %bitcast.95), channel_id=1, replica_groups=mesh['tile'=4,'dp'=8] {'tile','dp'}, use_global_device_ids=true, to_apply=%region_8.9 | all-reduce | flops 2818 | bytes 22544 | tf_op jit(solution)/shard_map/psum | solution.py:224
  1560.1 66.4 %all-reduce.15.cloned.1.call-done = f32[1,1600,1024]{2,1,0:T(8,128)} async-done(((f32[1,1600,1024]{2,1,0:T(8,128)}), f32[1,1600,1024]{2,1,0:T(8,128)}) %all-reduce.15.cloned.1.call-update) | async-done | bytes 6553616 | tf_op jit(solution)/shard_map/psum | solution.py:222
  1626.4 5.1 multiply_reduce_fusion
  1632.9 22.0 %psum.52 = f32[]{:T(128)} all-reduce(f32[]{:T(128)} %multiply_reduce_fusion), channel_id=1, replica_groups=mesh['tile'=4,'dp'=8] {'dp'}, use_global_device_ids=true, to_apply=%region_18.19 | all-reduce | flops 1 | bytes 8 | tf_op jit(solution)/shard_map/psum | solution.py:227
  1659.0 17.3 %multiply_subtract_fusion = (f32[1,1600,1024]{2,1,0:T(8,128)}, f32[1,1600,1024]{2,1,0:T(8,128)}, f32[1,1600,1024]{2,1,0:T(8,128)}) fusion(f32[1,1600,1024]{2,1,0:T(8,128)} %param.24, f32[]{:T(128)} %bitcast.97, f32[1,1600,1024]{2,1,0:T(8,128)} %all-reduce.15.cloned.1.call-done, f32[]{:T(128)} %div.177, f32[1,1600,1024]{2,1,0:T(8,128)} %param.26, ...), kind=kLoop, calls=%fused_computation.10 | loop fusion | flops 24576000 | bytes 45875208 | tf_op jit(solution)/shard_map/sub | solution.py:130
  (289 shorter events, 40.2 us)
Async XLA Ops:
  7.2 509.5 %all-gather.3.cloned.1.call-start = ((), (), s32[]{:S(2)}) async-start(), calls=%async_computation.3 | async-start | bytes 29491200 | tf_op jit(solution)/shard_map/all_gather | solution.py:166
  12.3 5.9 copy-start.7
  12.3 5.9 copy-start.19
  12.4 1487.3 %reduce-scatter.2.cloned.1.call-start = ((), (), s32[]{:S(2)}) async-start(), calls=%async_computation.1 | async-start | bytes 58982400 | tf_op jit(solution)/shard_map/reduce_scatter | solution.py:221
  13.0 93.6 %copy-start.9 = (f32[2,32]{1,0:T(2,128)}, f32[2,32]{1,0:T(2,128)S(1)}, u32[]{:S(2)}) copy-start(f32[2,32]{1,0:T(2,128)S(1)} %get-tuple-element.135) | copy-start | bytes 772
  13.2 92.8 %collective-permute-start.1 = (bf16[1,2,32,512]{3,2,1,0:T(8,128)(2,1)S(1)}, bf16[1,2,32,512]{3,2,1,0:T(8,128)(2,1)S(1)}, u32[]{:S(2)}, u32[]{:S(2)}) collective-permute-start(bf16[1,2,32,512]{3,2,1,0:T(8,128)(2,1)S(1)} %pad_maximum_fusion.12), channel_id=1, source_target_pairs={{8,0},{16,8},{24,16},{9,1},{17,9},{25,17},{10,2},{18,10},{26,18},{... | collective-permute-start | bytes 196616 | tf_op jit(solution)/shard_map/ppermute | solution.py:23
  14.5 91.5 %collective-permute-start = (bf16[1,2,32,512]{3,2,1,0:T(8,128)(2,1)S(1)}, bf16[1,2,32,512]{3,2,1,0:T(8,128)(2,1)S(1)}, u32[]{:S(2)}, u32[]{:S(2)}) collective-permute-start(bf16[1,2,32,512]{3,2,1,0:T(8,128)(2,1)S(1)} %pad_maximum_fusion.12), channel_id=1, source_target_pairs={{0,8},{8,16},{16,24},{1,9},{9,17},{17,25},{2,10},{10,18},{18,26},{... | collective-permute-start | bytes 196616 | tf_op jit(solution)/shard_map/ppermute | solution.py:21
  530.1 56.6 %collective-permute-start.3 = (bf16[1,2,32,512]{3,2,1,0:T(8,128)(2,1)S(1)}, bf16[1,2,32,512]{3,2,1,0:T(8,128)(2,1)S(1)}, u32[]{:S(2)}, u32[]{:S(2)}) collective-permute-start(bf16[1,2,32,512]{3,2,1,0:T(8,128)(2,1)S(1)} %pad_maximum_fusion.13), channel_id=1, source_target_pairs={{8,0},{16,8},{24,16},{9,1},{17,9},{25,17},{10,2},{18,10},{26,18},{... | collective-permute-start | bytes 196616 | tf_op jit(solution)/shard_map/ppermute | solution.py:23
  531.4 55.3 %collective-permute-start.2 = (bf16[1,2,32,512]{3,2,1,0:T(8,128)(2,1)S(1)}, bf16[1,2,32,512]{3,2,1,0:T(8,128)(2,1)S(1)}, u32[]{:S(2)}, u32[]{:S(2)}) collective-permute-start(bf16[1,2,32,512]{3,2,1,0:T(8,128)(2,1)S(1)} %pad_maximum_fusion.13), channel_id=1, source_target_pairs={{0,8},{8,16},{16,24},{1,9},{9,17},{17,25},{2,10},{10,18},{18,26},{... | collective-permute-start | bytes 196616 | tf_op jit(solution)/shard_map/ppermute | solution.py:21
  601.1 1.8 copy-start.15
  602.8 41.9 %copy-start.3 = (f32[1,2,32,256]{3,2,1,0:T(8,128)}, f32[1,2,32,256]{3,2,1,0:T(8,128)S(1)}, u32[]{:S(2)}) copy-start(f32[1,2,32,256]{3,2,1,0:T(8,128)S(1)} %get-tuple-element.37) | copy-start | bytes 196612
  606.1 26.7 %collective-permute-start.5 = (bf16[1,2,32,1024]{3,2,1,0:T(8,128)(2,1)S(1)}, bf16[1,2,32,1024]{3,2,1,0:T(8,128)(2,1)S(1)}, u32[]{:S(2)}, u32[]{:S(2)}) collective-permute-start(bf16[1,2,32,1024]{3,2,1,0:T(8,128)(2,1)S(1)} %fusion.25), channel_id=1, source_target_pairs={{8,0},{16,8},{24,16},{9,1},{17,9},{25,17},{10,2},{18,10},{26,18},{... | collective-permute-start | bytes 393224 | tf_op jit(solution)/shard_map/ppermute | solution.py:23
  607.4 25.4 %collective-permute-start.4 = (bf16[1,2,32,1024]{3,2,1,0:T(8,128)(2,1)S(1)}, bf16[1,2,32,1024]{3,2,1,0:T(8,128)(2,1)S(1)}, u32[]{:S(2)}, u32[]{:S(2)}) collective-permute-start(bf16[1,2,32,1024]{3,2,1,0:T(8,128)(2,1)S(1)} %fusion.25), channel_id=1, source_target_pairs={{0,8},{8,16},{16,24},{1,9},{9,17},{17,25},{2,10},{10,18},{18,26},{... | collective-permute-start | bytes 393224 | tf_op jit(solution)/shard_map/ppermute | solution.py:21
  633.8 11.0 copy-start.6
  681.5 944.9 %all-reduce.15.cloned.1.call-start = ((), (), s32[]{:S(2)}) async-start(), calls=%async_computation.2 | async-start | bytes 13107200 | tf_op jit(solution)/shard_map/psum | solution.py:222
  683.5 9.1 collective-permute-start.7
  684.8 7.8 collective-permute-start.6
  1503.7 12.9 copy-start.10
  1560.0 97.7 %copy-start.8 = (f32[2,1,1024]{2,1,0:T(1,128)S(1)}, f32[2,1,1024]{2,1,0:T(1,128)}, u32[]{:S(2)}) copy-start(f32[2,1,1024]{2,1,0:T(1,128)} %param.27) | copy-start | bytes 24580
  1560.0 97.7 %copy-start.13 = (f32[2,1,1024]{2,1,0:T(1,128)S(1)}, f32[2,1,1024]{2,1,0:T(1,128)}, u32[]{:S(2)}) copy-start(f32[2,1,1024]{2,1,0:T(1,128)} %param.29) | copy-start | bytes 24580
  1560.0 97.7 %copy-start.14 = (f32[2,1,1024]{2,1,0:T(1,128)S(1)}, f32[2,1,1024]{2,1,0:T(1,128)}, u32[]{:S(2)}) copy-start(f32[2,1,1024]{2,1,0:T(1,128)} %param.28) | copy-start | bytes 24580
  1560.0 98.3 %copy-start.12 = (f32[3,256]{1,0:T(4,128)S(1)}, f32[3,256]{1,0:T(4,128)}, u32[]{:S(2)}) copy-start(f32[3,256]{1,0:T(4,128)} %param.30) | copy-start | bytes 9220
  1560.0 98.3 %copy-start.16 = (f32[3,256]{1,0:T(4,128)S(1)}, f32[3,256]{1,0:T(4,128)}, u32[]{:S(2)}) copy-start(f32[3,256]{1,0:T(4,128)} %param.32) | copy-start | bytes 9220
  1560.0 98.3 %copy-start.17 = (f32[3,256]{1,0:T(4,128)S(1)}, f32[3,256]{1,0:T(4,128)}, u32[]{:S(2)}) copy-start(f32[3,256]{1,0:T(4,128)} %param.31) | copy-start | bytes 9220
  (7 other events, 7.4 us)
Sparse Core Ops, SparseCore 0:
  12.5 504.1 all-gather.2
  681.6 817.9 reduce-scatter.1
  1502.0 124.3 all-reduce.14
where the time goes:
time: 1690 us
  waiting for transfers between devices  1270 us (75%)
  blocking collectives  149 us (9%)
  matrix products  100 us (6%)
  local copies, waits for them, and re-layouts  76.5 us (5%)
  other arithmetic  41.9 us (2%)
  between operations  32.4 us (2%)
  starting transfers between devices  19.7 us (1%)
    reduce_scatter x1, waiting for transfers between devices, per_device(): lax.psum_scatter(grad_kernels, 'dp', scatter_dimension=1, tiled=True)  794 us
    all_gather x1, waiting for transfers between devices, per_device(): lax.all_gather(kernels[layer_no].astype(jnp.bfloat16), 'dp', axis=0, tile...  408 us
    psum x1, blocking collectives, per_device(): count = jnp.maximum(lax.psum(jnp.sum(valid), ('tile', 'dp')), 1.0)  85.6 us
    psum x1, waiting for transfers between devices, per_device(): shard = lax.psum(shard, 'tile')  66.4 us
    dot_general x2, matrix products, layer_backward(): lax.dot_general(unfold(padded, rows, columns), gates_low.reshape(-1, gate...  55.1 us
    transpose x2, local copies, waits for them, and re-layouts, layer_backward(): flipped.transpose(0, 1, 3, 2).reshape(KERNEL * KERNEL * gate_dim, in_dim)  52.3 us
    psum x1, blocking collectives, per_device(): lax.psum((grad_norms, grad_ends, grad_head, loss_sum), ('tile', 'dp'))  41.4 us
  transfers between devices with their start and end apart: 11, of which 3 were waited for; matrix products, arithmetic and copies ran while one was open for 6% of the time, Pallas kernels for 0%

commit v1 on v0

--- a/solution.py
+++ b/solution.py
@@ -219,7 +219,7 @@
     grad_ends = jnp.stack([grad_lift_weight, grad_lift_bias, grad_head_weight])
     grad_kernels = jnp.stack(kernel_grads)
     shard = lax.psum_scatter(grad_kernels, "dp", scatter_dimension=1, tiled=True)
-    shard = lax.psum(shard, "tile")
+    shard = jnp.sum(lax.all_gather(shard, "tile"), axis=0)
     local_square = jnp.sum(shard * shard)
     grad_norms, grad_ends, grad_head, loss_sum = lax.psum(
         (grad_norms, grad_ends, grad_head, loss_sum), ("tile", "dp")

time: 1690 us -> 1740 us (1.030)
  waiting for transfers between devices: 1270 us -> 1320 us
    all_gather x0 -> x1, waiting for transfers between devices: none -> 91 us  [per_device(): shard = jnp.sum(lax.all_gather(shard, 'tile'), axis=0)]
    psum x1 -> x0, waiting for transfers between devices: 66.4 us -> none  [per_device(): shard = lax.psum(shard, 'tile')]
    reduce_scatter x1, waiting for transfers between devices: 794 us -> 818 us  [per_device(): lax.psum_scatter(grad_kernels, 'dp', scatter_dimension=1, tiled=True)]
  transfers between devices with their start and end apart: 11 -> 11, of which waited for: 3 -> 3; matrix products, arithmetic and copies ran while one was open for 6% -> 5% of each run, Pallas kernels for 0% -> 0%
where the time goes in v1:
time: 1740 us
  waiting for transfers between devices  1320 us (76%)
  blocking collectives  150 us (9%)
  matrix products  104 us (6%)
  local copies, waits for them, and re-layouts  61.5 us (4%)
  other arithmetic  56.1 us (3%)
  between operations  32.6 us (2%)
  starting transfers between devices  18.4 us (1%)
    reduce_scatter x1, waiting for transfers between devices, per_device(): lax.psum_scatter(grad_kernels, 'dp', scatter_dimension=1, tiled=True)  818 us
    all_gather x1, waiting for transfers between devices, per_device(): lax.all_gather(kernels[layer_no].astype(jnp.bfloat16), 'dp', axis=0, tile...  408 us
    all_gather x1, waiting for transfers between devices, per_device(): shard = jnp.sum(lax.all_gather(shard, 'tile'), axis=0)  91 us
    psum x1, blocking collectives, per_device(): count = jnp.maximum(lax.psum(jnp.sum(valid), ('tile', 'dp')), 1.0)  85.6 us
    dot_general x2, matrix products, layer_backward(): lax.dot_general(unfold(padded, rows, columns), gates_low.reshape(-1, gate...  55.1 us
    transpose x2, local copies, waits for them, and re-layouts, layer_backward(): flipped.transpose(0, 1, 3, 2).reshape(KERNEL * KERNEL * gate_dim, in_dim)  52.3 us
    psum x1, blocking collectives, per_device(): lax.psum((grad_norms, grad_ends, grad_head, loss_sum), ('tile', 'dp'))  41.9 us
  transfers between devices with their start and end apart: 11, of which 3 were waited for; matrix products, arithmetic and copies ran while one was open for 5% of the time, Pallas kernels for 0%

profile of v1, /device:TPU:0, one launch (start us, length us, event | category | flops | bytes accessed | tf_op | source)
XLA Modules:
  0.0 1739.9 jit_solution(17214514871701624718)
XLA Ops:
  7.2 5.1 convert_element_type.95
  13.2 1.3 collective-permute-start.1
  14.5 3.0 collective-permute-start
  18.9 85.6 %psum.43 = f32[]{:T(128)} all-reduce(f32[]{:T(128)} %get-tuple-element.65), channel_id=1, replica_groups=mesh['tile'=4,'dp'=8] {'tile','dp'}, use_global_device_ids=true, to_apply=%region_10.11 | all-reduce | flops 1 | bytes 8 | tf_op jit(solution)/shard_map/psum | solution.py:159
  108.5 408.1 %all-gather.5.cloned.1.call-done = bf16[1,12800,1024]{2,1,0:T(8,128)(2,1)} async-done(((bf16[1,1600,1024]{2,1,0:T(8,128)(2,1)}), bf16[1,12800,1024]{2,1,0:T(8,128)(2,1)}) %all-gather.5.cloned.1.call-update) | async-done | bytes 26214416 | tf_op jit(solution)/shard_map/all_gather | solution.py:166
  516.7 10.8 fusion.3
  530.1 1.3 collective-permute-start.3
  531.4 3.0 collective-permute-start.2
  534.4 18.4 %reverse_bitcast_fusion = bf16[5,5,1024,512]{2,3,1,0:T(8,128)(2,1)} fusion(bf16[5,5,512,1024]{3,2,1,0:T(8,128)(2,1)} %bitcast.219), kind=kLoop, calls=%fused_computation.6 | loop fusion | bytes 52428800 | tf_op jit(solution)/shard_map/transpose | solution.py:93
  552.8 33.9 %copy.36 = bf16[5,5,1024,512]{3,2,1,0:T(8,128)(2,1)} copy(bf16[5,5,1024,512]{2,3,1,0:T(8,128)(2,1)} %reverse_bitcast_fusion) | data formatting | bytes 52428800 | tf_op jit(solution)/shard_map/transpose | solution.py:93
  588.8 10.8 fusion.1
  607.9 3.8 collective-permute-start.4
  611.7 21.6 %fusion.11 = f32[12800,1024,1]{1,0,2:T(8,128)} fusion(bf16[1,2,32,12800]{3,2,1,0:T(8,128)(2,1)} %copy-done, bf16[1,2,32,1024]{3,2,1,0:T(8,128)(2,1)S(1)} %fusion.25), kind=kOutput, calls=%fused_computation.17 | convolution fusion | flops 1677721600 | bytes 54198272 | tf_op jit(solution)/shard_map/dot_general | solution.py:109
  634.4 10.8 fusion.13
  649.1 33.5 %fusion = f32[1,12800,1024]{2,1,0:T(8,128)} fusion(f32[12800,1024,1]{1,0,2:T(8,128)} %fusion.11, bf16[1,2,32,12800]{3,2,1,0:T(8,128)(2,1)S(1)} %copy-done.2, bf16[1,2,32,1024]{3,2,1,0:T(8,128)(2,1)S(1)} %fusion.27), kind=kOutput, calls=%fused_computation.1 | convolution fusion | flops 1690828800 | bytes 106627072 | tf_op jit(solution)/shard_map/dot_general | solution.py:109
  682.7 818.0 %reduce-scatter.2.cloned.1.call-done = f32[1,1600,1024]{2,1,0:T(8,128)} async-done(((f32[1,12800,1024]{2,1,0:T(8,128)}), f32[1,1600,1024]{2,1,0:T(8,128)}) %reduce-scatter.2.cloned.1.call-update) | async-done | bytes 6553616 | tf_op jit(solution)/shard_map/reduce_scatter | solution.py:221
  1504.0 3.3 collective-permute-start.6
  1511.6 16.9 fusion.16
  1528.7 41.9 %all-reduce.12 = (f32[]{:T(128)}, f32[2,1,1024]{2,1,0:T(1,128)S(1)}, f32[3,256]{1,0:T(4,128)S(1)}, f32[1]{0:T(128)}) all-reduce(f32[]{:T(128)S(6)} %add.408, f32[2,1,1024]{2,1,0:T(1,128)S(1)} %pad_maximum_fusion.14, f32[3,256]{1,0:T(4,128)S(1)} %pad_maximum_fusion.15, f32[1]{0:T(128)} %bitcast.95), channel_id=1, replica_groups=mesh['tile'=4,'dp'=8] {'tile','dp'}, use_global_device_ids=true, to_apply=%region_8.9 | all-reduce | flops 2818 | bytes 22544 | tf_op jit(solution)/shard_map/psum | solution.py:224
  1572.5 91.0 %all-gather.7.cloned.1.call-done = f32[4,1600,1024]{2,1,0:T(8,128)} async-done(((f32[1,1600,1024]{2,1,0:T(8,128)}), f32[4,1600,1024]{2,1,0:T(8,128)}) %all-gather.7.cloned.1.call-update) | async-done | bytes 26214416 | tf_op jit(solution)/shard_map/all_gather | solution.py:222
  1663.4 14.3 reduce.16
  1677.7 5.1 multiply_reduce_fusion
  1684.2 22.0 %psum.44 = f32[]{:T(128)} all-reduce(f32[]{:T(128)} %multiply_reduce_fusion), channel_id=1, replica_groups=mesh['tile'=4,'dp'=8] {'dp'}, use_global_device_ids=true, to_apply=%region_18.19 | all-reduce | flops 1 | bytes 8 | tf_op jit(solution)/shard_map/psum | solution.py:227
  1709.1 17.3 multiply_subtract_fusion
  (296 shorter events, 26.3 us)
Async XLA Ops:
  7.2 509.5 %all-gather.5.cloned.1.call-start = ((), (), s32[]{:S(2)}) async-start(), calls=%async_computation.2 | async-start | bytes 29491200 | tf_op jit(solution)/shard_map/all_gather | solution.py:166
  12.4 1488.3 %reduce-scatter.2.cloned.1.call-start = ((), (), s32[]{:S(2)}) async-start(), calls=%async_computation.1 | async-start | bytes 58982400 | tf_op jit(solution)/shard_map/reduce_scatter | solution.py:221
  13.0 93.6 %copy-start.9 = (f32[2,32]{1,0:T(2,128)}, f32[2,32]{1,0:T(2,128)S(1)}, u32[]{:S(2)}) copy-start(f32[2,32]{1,0:T(2,128)S(1)} %get-tuple-element.135) | copy-start | bytes 772
  13.2 92.8 %collective-permute-start.1 = (bf16[1,2,32,512]{3,2,1,0:T(8,128)(2,1)S(1)}, bf16[1,2,32,512]{3,2,1,0:T(8,128)(2,1)S(1)}, u32[]{:S(2)}, u32[]{:S(2)}) collective-permute-start(bf16[1,2,32,512]{3,2,1,0:T(8,128)(2,1)S(1)} %pad_maximum_fusion.12), channel_id=1, source_target_pairs={{8,0},{16,8},{24,16},{9,1},{17,9},{25,17},{10,2},{18,10},{26,18},{... | collective-permute-start | bytes 196616 | tf_op jit(solution)/shard_map/ppermute | solution.py:23
  14.5 91.5 %collective-permute-start = (bf16[1,2,32,512]{3,2,1,0:T(8,128)(2,1)S(1)}, bf16[1,2,32,512]{3,2,1,0:T(8,128)(2,1)S(1)}, u32[]{:S(2)}, u32[]{:S(2)}) collective-permute-start(bf16[1,2,32,512]{3,2,1,0:T(8,128)(2,1)S(1)} %pad_maximum_fusion.12), channel_id=1, source_target_pairs={{0,8},{8,16},{16,24},{1,9},{9,17},{17,25},{2,10},{10,18},{18,26},{... | collective-permute-start | bytes 196616 | tf_op jit(solution)/shard_map/ppermute | solution.py:21
  530.1 56.6 %collective-permute-start.3 = (bf16[1,2,32,512]{3,2,1,0:T(8,128)(2,1)S(1)}, bf16[1,2,32,512]{3,2,1,0:T(8,128)(2,1)S(1)}, u32[]{:S(2)}, u32[]{:S(2)}) collective-permute-start(bf16[1,2,32,512]{3,2,1,0:T(8,128)(2,1)S(1)} %pad_maximum_fusion.13), channel_id=1, source_target_pairs={{8,0},{16,8},{24,16},{9,1},{17,9},{25,17},{10,2},{18,10},{26,18},{... | collective-permute-start | bytes 196616 | tf_op jit(solution)/shard_map/ppermute | solution.py:23
  531.4 55.3 %collective-permute-start.2 = (bf16[1,2,32,512]{3,2,1,0:T(8,128)(2,1)S(1)}, bf16[1,2,32,512]{3,2,1,0:T(8,128)(2,1)S(1)}, u32[]{:S(2)}, u32[]{:S(2)}) collective-permute-start(bf16[1,2,32,512]{3,2,1,0:T(8,128)(2,1)S(1)} %pad_maximum_fusion.13), channel_id=1, source_target_pairs={{0,8},{8,16},{16,24},{1,9},{9,17},{17,25},{2,10},{10,18},{18,26},{... | collective-permute-start | bytes 196616 | tf_op jit(solution)/shard_map/ppermute | solution.py:21
  602.8 42.4 %copy-start.3 = (f32[1,2,32,256]{3,2,1,0:T(8,128)}, f32[1,2,32,256]{3,2,1,0:T(8,128)S(1)}, u32[]{:S(2)}) copy-start(f32[1,2,32,256]{3,2,1,0:T(8,128)S(1)} %get-tuple-element.37) | copy-start | bytes 196612
  606.6 26.7 %collective-permute-start.5 = (bf16[1,2,32,1024]{3,2,1,0:T(8,128)(2,1)S(1)}, bf16[1,2,32,1024]{3,2,1,0:T(8,128)(2,1)S(1)}, u32[]{:S(2)}, u32[]{:S(2)}) collective-permute-start(bf16[1,2,32,1024]{3,2,1,0:T(8,128)(2,1)S(1)} %fusion.25), channel_id=1, source_target_pairs={{8,0},{16,8},{24,16},{9,1},{17,9},{25,17},{10,2},{18,10},{26,18},{... | collective-permute-start | bytes 393224 | tf_op jit(solution)/shard_map/ppermute | solution.py:23
  607.9 25.4 %collective-permute-start.4 = (bf16[1,2,32,1024]{3,2,1,0:T(8,128)(2,1)S(1)}, bf16[1,2,32,1024]{3,2,1,0:T(8,128)(2,1)S(1)}, u32[]{:S(2)}, u32[]{:S(2)}) collective-permute-start(bf16[1,2,32,1024]{3,2,1,0:T(8,128)(2,1)S(1)} %fusion.25), channel_id=1, source_target_pairs={{0,8},{8,16},{16,24},{1,9},{9,17},{17,25},{2,10},{10,18},{18,26},{... | collective-permute-start | bytes 393224 | tf_op jit(solution)/shard_map/ppermute | solution.py:21
  634.4 10.9 copy-start.16
  634.4 11.6 copy-start.6
  682.6 980.8 %all-gather.7.cloned.1.call-start = ((), (), s32[]{:S(2)}) async-start(), calls=%async_computation.3 | async-start | bytes 32768000 | tf_op jit(solution)/shard_map/all_gather | solution.py:222
  1500.7 9.9 copy-start.17
  1500.7 9.9 copy-start.18
  1502.7 7.9 collective-permute-start.7
  1504.0 6.6 collective-permute-start.6
  1511.6 16.9 copy-start.10
  1709.0 17.4 copy-start.8
  1709.0 17.4 copy-start.13
  1709.0 17.4 copy-start.14
  1709.0 18.0 %copy-start.12 = (f32[3,256]{1,0:T(4,128)S(1)}, f32[3,256]{1,0:T(4,128)}, u32[]{:S(2)}) copy-start(f32[3,256]{1,0:T(4,128)} %param.30) | copy-start | bytes 9220
  1709.1 18.0 %copy-start.19 = (f32[3,256]{1,0:T(4,128)S(1)}, f32[3,256]{1,0:T(4,128)}, u32[]{:S(2)}) copy-start(f32[3,256]{1,0:T(4,128)} %param.32) | copy-start | bytes 9220
  1709.1 18.0 %copy-start.20 = (f32[3,256]{1,0:T(4,128)S(1)}, f32[3,256]{1,0:T(4,128)}, u32[]{:S(2)}) copy-start(f32[3,256]{1,0:T(4,128)} %param.31) | copy-start | bytes 9220
  (10 other events, 21.0 us)
Sparse Core Ops, SparseCore 0:
  12.5 504.1 all-gather.4
  682.7 817.8 reduce-scatter.1
  1502.2 161.1 all-gather.6
